TPU v7x, 32 devices: a whole 2x2x4 slice. The times are simulated.
32 devices in a mesh: gx: 8 (over y, x, core), gy: 4 (over z).
Axes of the slice: x: 2, y: 2, z: 4, core: 2. Of those that a mesh axis runs over, the one named last changes fastest.
Arguments:
- dual_distributions: float32 [26, 4, 128, 512], P(None, None, 'gx', 'gy'), may hold values from -6 to 6
- primal_fluid_rho: float32 [4, 128, 512], P(None, 'gx', 'gy'), may hold values from 0.8 to 1.2
- forward_flow_speed: float32 [3, 4, 128, 512], P(None, None, 'gx', 'gy'), may hold values from -0.15 to 0.15
- primal_kelvin_values: float32 [4, 128, 512], P(None, 'gx', 'gy'), may hold values from 0.5 to 1.5
- obstacle_mask: int32 [4, 128, 512], P(None, 'gx', 'gy'), may hold values 0 or 1
- objective_surface_mask: int32 [4, 128, 512], P(None, 'gx', 'gy'), may hold values 0 or 1
- pillar_porosity: float32 [128, 512], P('gx', 'gy'), may hold values from 0 to 1
- pillar_design_patch: int32 [128, 512], P('gx', 'gy'), may hold values from 0 to 15, as said below
- patch_holder: int32 [512, 1], P(('gx', 'gy')), may hold values from 0 to 7; in each aligned block of 16 rows (0 to 15, 16 to 31, ...) at most 4 rows name the same one
Outputs:
- adjoint_next: float32 [26, 4, 128, 512], P(None, None, 'gx', 'gy')
- refreshed_owner_tiles: float32 [1024, 128], P(('gx', 'gy'))
Inputs may be any that keep to these rules, and one draw needn't show every extreme that they name: `pillar_design_patch`: on each device, every local block number names exactly 128 of its columns. `patch_holder`: among the 16 blocks of one device, at most 4 have the same owner.
All inputs are finite; a program needn't handle non-finite values. No bound on the sum of `obstacle_mask` or of `objective_surface_mask` on one device may be relied on, other than what follows from the above.
Results may differ from a plain program's by a relative error of at most 0.0003.
Values sent between devices are 32-bit elements; how exact they have to be, the bound alone decides.
A program may use at most 64 MiB of HBM per device.

v0:
```python
import functools

import jax
import jax.numpy as jnp
from jax import lax
from jax.experimental import pallas as pl
from jax.experimental.pallas import tpu as pltpu
from jax.sharding import PartitionSpec as P

STEPS = 6
TILE = 128

VELOCITIES = (
    (0, 0, 0),
    (1, 0, 0),
    (-1, 0, 0),
    (0, 1, 0),
    (0, -1, 0),
    (0, 0, 1),
    (0, 0, -1),
    (1, 1, 0),
    (-1, -1, 0),
    (1, -1, 0),
    (-1, 1, 0),
    (1, 0, 1),
    (-1, 0, -1),
    (1, 0, -1),
    (-1, 0, 1),
    (0, 1, 1),
    (0, -1, -1),
    (0, 1, -1),
    (0, -1, 1),
)
W0, W1, W2 = 1.0 / 3.0, 1.0 / 18.0, 1.0 / 36.0
V0, V1 = 0.25, 0.125
FLOW = 19
POPS = 26
OMEGA_FLOW = 1.6
CONDUCT_RATE = 1.2
SOURCE_RATE = 0.5
HEAT_RATE = 0.1
STEP_SIZE = 0.1

DIRS = ((-1, 0), (1, 0), (0, -1), (0, 1), (-1, -1), (1, -1), (-1, 1), (1, 1))
MESH = pl.DeviceIdType.MESH
PAD = 8


def velocity(pop):
    return VELOCITIES[pop if pop < FLOW else pop - FLOW]


def opposite(pop):
    base = 0 if pop < FLOW else FLOW
    within = pop - base
    if within == 0:
        return pop
    return base + (within + 1 if within % 2 == 1 else within - 1)


def moving(axis, sign):
    return [pop for pop in range(POPS) if velocity(pop)[axis] == sign]


XPOPS = (moving(0, 1), moving(0, -1))
YPOPS = (moving(1, 1), moving(1, -1))


def split3(value):
    high = value.astype(jnp.bfloat16)
    rest = value - high.astype(jnp.float32)
    middle = rest.astype(jnp.bfloat16)
    low = (rest - middle.astype(jnp.float32)).astype(jnp.bfloat16)
    return high, middle, low


def body(
    sizes,
    f_hbm,
    rho_ref,
    speed_ref,
    kelvin_ref,
    obstacle_ref,
    surface_ref,
    porosity_ref,
    patch_ref,
    holder_ref,
    out_hbm,
    tiles_ref,
    state,
    const,
    acc,
    xsend,
    xrecv,
    ysend,
    yrecv,
    csend,
    crecv,
    yhalo,
    hot,
    label_rows,
    flip_a,
    flip_b,
    column,
    mirror,
    outgoing,
    received,
    load_sem,
    store_sem,
    send_sem,
    recv_sem,
    msend_sem,
    mrecv_sem,
    asend_sem,
    arecv_sem,
):
    nx, ny, height, ex, ey, blocks, cap = sizes
    i = lax.axis_index("gx")
    j = lax.axis_index("gy")
    tiles_of = ex // 8

    load = pltpu.make_async_copy(f_hbm, state.at[0, :, :, pl.ds(PAD, ex), :], load_sem)
    load.start()

    barrier = pltpu.get_barrier_semaphore()

    def inside(di, dj):
        a, b = i + di, j + dj
        return (a >= 0) & (a < nx) & (b >= 0) & (b < ny)

    xrecv[...] = jnp.zeros(xrecv.shape, jnp.float32)
    yrecv[...] = jnp.zeros(yrecv.shape, jnp.float32)
    crecv[...] = jnp.zeros(crecv.shape, jnp.float32)
    acc[...] = jnp.zeros(acc.shape, jnp.float32)

    mirrors = ((nx - 1 - i, j), (i, ny - 1 - j), (nx - 1 - i, ny - 1 - j))
    for dx, dy in DIRS:
        @pl.when(inside(dx, dy))
        def _():
            pl.semaphore_signal(barrier, inc=1, device_id=(i + dx, j + dy), device_id_type=MESH)
    for d in range(1, nx):
        pl.semaphore_signal(barrier, inc=1, device_id=(lax.rem(i + d, nx), j), device_id_type=MESH)
    for target in mirrors:
        pl.semaphore_signal(barrier, inc=1, device_id=target, device_id_type=MESH)

    lane = lax.broadcasted_iota(jnp.int32, (8, ey), 1)

    for z in range(height):
        fluid = 1.0 - obstacle_ref[z].astype(jnp.float32)
        for axis in range(3):
            const[axis, z] = speed_ref[axis, z] * fluid
        const[3, z] = 4.0 * CONDUCT_RATE * kelvin_ref[z] / rho_ref[z]
        const[4, z] = SOURCE_RATE * surface_ref[z].astype(jnp.float32)
        const[5, z] = fluid

    wide = 1 + (i > 0).astype(jnp.int32) + (i < nx - 1).astype(jnp.int32)
    deep = 1 + (j > 0).astype(jnp.int32) + (j < ny - 1).astype(jnp.int32)
    pl.semaphore_wait(barrier, wide * deep - 1 + nx - 1 + len(mirrors))
    load.wait()

    def rim_copy(par, k):
        dx, dy = DIRS[k]
        if k < 2:
            src, dst = xsend.at[par, k], xrecv.at[par, k]
        elif k < 4:
            src, dst = ysend.at[par, k - 2], yrecv.at[par, k - 2]
        else:
            src, dst = csend.at[par, k - 4], crecv.at[par, k - 4]
        return pltpu.make_async_remote_copy(
            src_ref=src,
            dst_ref=dst,
            send_sem=send_sem.at[par, k],
            recv_sem=recv_sem.at[par, k],
            device_id=(i + dx, j + dy),
            device_id_type=MESH,
        )

    def send_rim(par):
        for side in range(2):
            row = PAD if side == 0 else PAD + ex - 1
            for p, pop in enumerate(XPOPS[side]):
                for z in range(height):
                    q = p * height + z
                    xsend[par, side, q : q + 1, :] = state[par, pop, z, row : row + 1, :]
        for k in range(2):
            @pl.when(inside(*DIRS[k]))
            def _():
                rim_copy(par, k).start()
        for side in range(2):
            for rt in range(tiles_of):
                packed = jnp.zeros((8, ey), jnp.float32)
                for p, pop in enumerate(YPOPS[side]):
                    for z in range(height):
                        q = p * height + z
                        value = state[par, pop, z, PAD + rt * 8 : PAD + rt * 8 + 8, :]
                        shift = q if side == 0 else (q + 1) % ey
                        if shift:
                            value = pltpu.roll(value, shift, 1)
                        packed = jnp.where(lane == q, value, packed)
                ysend[par, side, rt * 8 : rt * 8 + 8, :] = packed
                for k in range(4, 8):
                    dx, dy = DIRS[k]
                    if (0 if dy < 0 else 1) == side:
                        if dx < 0 and rt == 0:
                            csend[par, k - 4] = packed[0:1, :]
                        if dx > 0 and rt == tiles_of - 1:
                            csend[par, k - 4] = packed[7:8, :]
        for k in range(4, 8):
            @pl.when(inside(*DIRS[k]))
            def _():
                rim_copy(par, k).start()
        for k in range(2, 4):
            @pl.when(inside(*DIRS[k]))
            def _():
                rim_copy(par, k).start()

    def take_rim(par):
        for k in range(8):
            dx, dy = DIRS[k]

            @pl.when(inside(dx, dy))
            def _():
                rim_copy(par, k).wait_send()

            @pl.when(inside(-dx, -dy))
            def _():
                rim_copy(par, k).wait_recv()
        for side in range(2):
            row = PAD + ex if side == 0 else PAD - 1
            for p, pop in enumerate(XPOPS[side]):
                for z in range(height):
                    q = p * height + z
                    state[par, pop, z, row : row + 1, :] = xrecv[par, side, q : q + 1, :]
            yhalo[side, PAD : PAD + ex, :] = yrecv[par, side]
        for k in range(4, 8):
            dx, dy = DIRS[k]
            row = PAD + ex if dx < 0 else PAD - 1
            yhalo[0 if dy < 0 else 1, row : row + 1, :] = crecv[par, k - 4]

    def collide(par, z, rt):
        start = PAD + rt * 8

        def pull(pop):
            cx, cy, cz = velocity(pop)
            zz = z + cz
            if zz < 0 or zz >= height:
                return state[par, opposite(pop), z, start : start + 8, :]
            value = state[par, pop, zz, start + cx : start + cx + 8, :]
            if cy:
                side = 0 if cy == 1 else 1
                q = YPOPS[side].index(pop) * height + zz
                edge = yhalo[side, start + cx : start + cx + 8, :]
                last = ey - 1 if cy == 1 else 0
                shift = (last - q) % ey
                if shift:
                    edge = pltpu.roll(edge, shift, 1)
                value = pltpu.roll(value, (-cy) % ey, 1)
                value = jnp.where(lane == last, edge, value)
            return value

        rows = slice(rt * 8, rt * 8 + 8)
        ux, uy, uz = const[0, z, rows, :], const[1, z, rows, :], const[2, z, rows, :]
        coupling = const[3, z, rows, :]
        source = const[4, z, rows, :]
        fluid = const[5, z, rows, :] > 0.5

        b = [pull(FLOW + k) for k in range(7)]
        tsum = V0 * b[0] + V1 * ((b[1] + b[2]) + (b[3] + b[4]) + (b[5] + b[6]))
        qx, qy, qz = V1 * (b[1] - b[2]), V1 * (b[3] - b[4]), V1 * (b[5] - b[6])
        qu = qx * ux + qy * uy + qz * uz
        warm = CONDUCT_RATE * (tsum + 4.0 * qu) + source
        for k in range(7):
            state[1 - par, FLOW + k, z, start : start + 8, :] = (1.0 - CONDUCT_RATE) * b[k] + warm

        a = [pull(k) for k in range(FLOW)]
        sm = {k: a[k] + a[k + 1] for k in range(1, FLOW, 2)}
        df = {k: a[k] - a[k + 1] for k in range(1, FLOW, 2)}
        sx = (3.0 * W1) * df[1] + (3.0 * W2) * ((df[7] + df[9]) + (df[11] + df[13]))
        sy = (3.0 * W1) * df[3] + (3.0 * W2) * ((df[7] - df[9]) + (df[15] + df[17]))
        sz = (3.0 * W1) * df[5] + (3.0 * W2) * ((df[11] - df[13]) + (df[15] - df[17]))
        xy, xz, yz = sm[7] + sm[9], sm[11] + sm[13], sm[15] + sm[17]
        mass = W0 * a[0] + W1 * (sm[1] + sm[3] + sm[5]) + W2 * (xy + xz + yz)
        quad = (
            (ux * ux) * (W1 * sm[1] + W2 * (xy + xz))
            + (uy * uy) * (W1 * sm[3] + W2 * (xy + yz))
            + (uz * uz) * (W1 * sm[5] + W2 * (xz + yz))
            + (2.0 * W2)
            * (
                (ux * uy) * (sm[7] - sm[9])
                + (ux * uz) * (sm[11] - sm[13])
                + (uy * uz) * (sm[15] - sm[17])
            )
        )
        square = ux * ux + uy * uy + uz * uz
        scalar = mass * (1.0 - 1.5 * square) + 4.5 * quad
        base = OMEGA_FLOW * scalar - coupling * qu
        gx = OMEGA_FLOW * sx + coupling * qx
        gy = OMEGA_FLOW * sy + coupling * qy
        gz = OMEGA_FLOW * sz + coupling * qz
        along = {
            1: gx,
            3: gy,
            5: gz,
            7: gx + gy,
            9: gx - gy,
            11: gx + gz,
            13: gx - gz,
            15: gy + gz,
            17: gy - gz,
        }
        keep = 1.0 - OMEGA_FLOW

        def put(pop, value):
            state[1 - par, pop, z, start : start + 8, :] = value

        put(0, jnp.where(fluid, keep * a[0] + base, a[0]))
        for k in range(1, FLOW, 2):
            put(k, jnp.where(fluid, keep * a[k] + (base + along[k]), a[k + 1]))
            put(k + 1, jnp.where(fluid, keep * a[k + 1] + (base - along[k]), a[k]))
        return HEAT_RATE * tsum - rho_ref[z, rows, :] * (ux * sx + uy * sy + uz * sz)

    send_rim(0)

    number = lax.broadcasted_iota(jnp.int32, (blocks, ey), 0)
    below = (
        lax.broadcasted_iota(jnp.int32, (ey, ey), 0) < lax.broadcasted_iota(jnp.int32, (ey, ey), 1)
    ).astype(jnp.bfloat16)
    place = lax.broadcasted_iota(jnp.int32, (TILE, ey), 0).astype(jnp.float32)
    running = jnp.zeros((blocks, 1), jnp.float32)
    for x in range(ex):
        hits = (patch_ref[x : x + 1, :] == number).astype(jnp.float32)
        earlier = jnp.dot(
            hits.astype(jnp.bfloat16), below, preferred_element_type=jnp.float32
        )
        rank = jnp.sum(hits * (earlier + running), axis=0, keepdims=True)
        running = running + jnp.sum(hits, axis=1, keepdims=True)
        hot[:, x * ey : (x + 1) * ey] = (place == rank).astype(jnp.bfloat16)
        label_rows[:, x * ey : (x + 1) * ey] = hits

    def gathered(field):
        columns = jnp.concatenate(
            [
                label_rows[:, x * ey : (x + 1) * ey] * field[x : x + 1, :]
                for x in range(ex)
            ],
            axis=1,
        )
        parts = jnp.concatenate(split3(columns), axis=0)
        result = lax.dot_general(
            parts, hot[...], (((1,), (1,)), ((), ())), preferred_element_type=jnp.float32
        )
        return result[:blocks] + result[blocks : 2 * blocks] + result[2 * blocks :]

    design = gathered(porosity_ref[...])

    owner = jnp.broadcast_to(holder_ref[...], (blocks, TILE)).astype(jnp.float32)
    rows_of = lax.broadcasted_iota(jnp.int32, (blocks, TILE), 0)
    lanes_of = lax.broadcasted_iota(jnp.int32, (blocks, TILE), 1)
    diagonal = (rows_of == lanes_of).astype(jnp.float32)
    owner_row = jnp.sum(owner * diagonal, axis=0, keepdims=True)
    same = ((owner == owner_row) & (rows_of < lanes_of) & (lanes_of < blocks)).astype(jnp.float32)
    rank_row = jnp.sum(same, axis=0, keepdims=True)
    slot_row = owner_row * float(cap) + rank_row
    slots = nx * cap
    choose = (
        (lax.broadcasted_iota(jnp.int32, (slots, TILE), 0).astype(jnp.float32) == slot_row)
        & (lax.broadcasted_iota(jnp.int32, (slots, TILE), 1) < blocks)
    ).astype(jnp.bfloat16)

    def step(s, carry):
        par = lax.rem(s, 2)
        take_rim(par)
        for rt in range(tiles_of):
            sens = collide(par, 0, rt)
            for z in range(1, height):
                sens = sens + collide(par, z, rt)
            acc[rt * 8 : rt * 8 + 8, :] += sens

        @pl.when(s < STEPS - 1)
        def _():
            send_rim(1 - par)

        return carry

    lax.fori_loop(0, STEPS, step, 0)

    last = STEPS % 2
    store = pltpu.make_async_copy(state.at[last, :, :, pl.ds(PAD, ex), :], out_hbm, store_sem)
    store.start()

    column[...] = acc[...]

    def mirror_copy(m):
        return pltpu.make_async_remote_copy(
            src_ref=column,
            dst_ref=mirror.at[m],
            send_sem=msend_sem.at[m],
            recv_sem=mrecv_sem.at[m],
            device_id=mirrors[m],
            device_id_type=MESH,
        )

    for m in (2, 1, 0):
        mirror_copy(m).start()
    for m in range(3):
        mirror_copy(m).wait()
    for x in range(ex):
        flip_a[x : x + 1, :] = mirror[0, ex - 1 - x : ex - x, :]
        flip_b[x : x + 1, :] = mirror[2, ex - 1 - x : ex - x, :]
    reverse = (
        lax.broadcasted_iota(jnp.int32, (ey, ey), 0) + lax.broadcasted_iota(jnp.int32, (ey, ey), 1)
        == ey - 1
    ).astype(jnp.bfloat16)
    turned = jnp.dot(
        jnp.concatenate(split3(mirror[1] + flip_b[...]), axis=0),
        reverse,
        preferred_element_type=jnp.float32,
    )
    symmetric = (
        column[...] + flip_a[...] + (turned[:ex] + turned[ex : 2 * ex] + turned[2 * ex :])
    )
    sens = gathered(symmetric)
    spread = jnp.sqrt(jnp.mean(sens * sens, axis=1, keepdims=True) + 1e-06)
    fresh = jnp.clip(design - STEP_SIZE * sens / spread, 0.0, 1.0)
    padded = jnp.concatenate([fresh, jnp.zeros((TILE - blocks, TILE), jnp.float32)], axis=0)
    parts = jnp.concatenate(split3(padded), axis=1)
    sent = jnp.dot(choose, parts, preferred_element_type=jnp.float32)
    sent = sent[:, :TILE] + sent[:, TILE : 2 * TILE] + sent[:, 2 * TILE :]
    for o in range(nx):
        outgoing[o] = sent[o * cap : (o + 1) * cap, :]

    def owner_copy(d):
        target = lax.rem(i + d, nx)
        return pltpu.make_async_remote_copy(
            src_ref=outgoing.at[target],
            dst_ref=received.at[i],
            send_sem=asend_sem.at[d],
            recv_sem=arecv_sem.at[d],
            device_id=(target, j),
            device_id_type=MESH,
        )

    def arriving(d):
        origin = lax.rem(i + nx - d, nx)
        return pltpu.make_async_remote_copy(
            src_ref=outgoing.at[origin],
            dst_ref=received.at[origin],
            send_sem=asend_sem.at[d],
            recv_sem=arecv_sem.at[d],
            device_id=(origin, j),
            device_id_type=MESH,
        )

    for d in range(1, nx):
        owner_copy(d).start()
    received[i] = outgoing[i]
    for d in range(1, nx):
        owner_copy(d).wait_send()
        arriving(d).wait_recv()
    for o in range(nx):
        tiles_ref[o * cap : (o + 1) * cap, :] = received[o]
    store.wait()


def on_device(
    dual_distributions,
    primal_fluid_rho,
    forward_flow_speed,
    primal_kelvin_values,
    obstacle_mask,
    objective_surface_mask,
    pillar_porosity,
    pillar_design_patch,
    patch_holder,
):
    nx, ny = lax.axis_size("gx"), lax.axis_size("gy")
    pops, height, ex, ey = dual_distributions.shape
    blocks = ex * ey // TILE
    cap = max(2, 2 * blocks // nx)
    nxp, nyp = len(XPOPS[0]), len(YPOPS[0])
    f32 = jnp.float32
    vmem = pl.BlockSpec(memory_space=pltpu.VMEM)
    hbm = pl.BlockSpec(memory_space=pl.ANY)
    return pl.pallas_call(
        functools.partial(body, (nx, ny, height, ex, ey, blocks, cap)),
        out_shape=(
            jax.ShapeDtypeStruct(dual_distributions.shape, f32),
            jax.ShapeDtypeStruct((nx * cap, TILE), f32),
        ),
        in_specs=[hbm] + [vmem] * 8,
        out_specs=(hbm, vmem),
        scratch_shapes=[
            pltpu.VMEM((2, pops, height, ex + 2 * PAD, ey), f32),
            pltpu.VMEM((6, height, ex, ey), f32),
            pltpu.VMEM((ex, ey), f32),
            pltpu.VMEM((2, 2, nxp * height, ey), f32),
            pltpu.VMEM((2, 2, nxp * height, ey), f32),
            pltpu.VMEM((2, 2, ex, ey), f32),
            pltpu.VMEM((2, 2, ex, ey), f32),
            pltpu.VMEM((2, 4, 1, ey), f32),
            pltpu.VMEM((2, 4, 1, ey), f32),
            pltpu.VMEM((2, ex + 2 * PAD, ey), f32),
            pltpu.VMEM((TILE, ex * ey), jnp.bfloat16),
            pltpu.VMEM((blocks, ex * ey), f32),
            pltpu.VMEM((ex, ey), f32),
            pltpu.VMEM((ex, ey), f32),
            pltpu.VMEM((ex, ey), f32),
            pltpu.VMEM((3, ex, ey), f32),
            pltpu.VMEM((nx, cap, TILE), f32),
            pltpu.VMEM((nx, cap, TILE), f32),
            pltpu.SemaphoreType.DMA,
            pltpu.SemaphoreType.DMA,
            pltpu.SemaphoreType.DMA((2, 8)),
            pltpu.SemaphoreType.DMA((2, 8)),
            pltpu.SemaphoreType.DMA((3,)),
            pltpu.SemaphoreType.DMA((3,)),
            pltpu.SemaphoreType.DMA((nx,)),
            pltpu.SemaphoreType.DMA((nx,)),
        ],
        compiler_params=pltpu.CompilerParams(collective_id=0, has_side_effects=True),
    )(
        dual_distributions,
        primal_fluid_rho,
        forward_flow_speed,
        primal_kelvin_values,
        obstacle_mask,
        objective_surface_mask,
        pillar_porosity,
        pillar_design_patch,
        patch_holder,
    )


def solution(mesh):
    in_specs = (
        P(None, None, "gx", "gy"),
        P(None, "gx", "gy"),
        P(None, None, "gx", "gy"),
        P(None, "gx", "gy"),
        P(None, "gx", "gy"),
        P(None, "gx", "gy"),
        P("gx", "gy"),
        P("gx", "gy"),
        P(("gx", "gy"), None),
    )
    out_specs = (P(None, None, "gx", "gy"), P(("gx", "gy"), None))
    return jax.shard_map(
        on_device, mesh=mesh, in_specs=in_specs, out_specs=out_specs, check_vma=False
    )
```

profile of v0, /device:TPU:0, one launch (start us, length us, event | category | flops | bytes accessed | tf_op | source)
XLA Modules:
  0.0 43.2 jit_solution(13401744343512189110)
XLA Ops:
  0.6 1.3 %copy.11.holder_ref = s32[16,1]{1,0:T(8,128)} copy(s32[16,1]{0,1:T(1,128)} %param.17) | data formatting | bytes 128 | tf_op args[8]
  2.0 38.5 %shard_map.104 = (f32[26,4,16,128]{3,2,1,0:T(8,128)}, f32[32,128]{1,0:T(8,128)}) custom-call(f32[26,4,16,128]{3,2,1,0:T(8,128)} %f_hbm.1, f32[4,16,128]{2,1,0:T(8,128)} %rho_ref.1, f32[3,4,16,128]{3,2,1,0:T(8,128)} %speed_ref.1, f32[4,16,128]{2,1,0:T(8,128)} %kelvin_ref.1, s32[4,16,128]{2,1,0:T(8,128)} %obstacle_ref.1, s32[4,16,128]{2,1,0:T(8,128)} %surface_ref.1, ...), custom_call_target="tpu_custom_call" | custom-call | tf_op jit(solution)/shard_map/pallas_call | solution.py:484
  40.5 0.0 copy-start
  40.5 2.1 %copy.14 = f32[26,4,16,128]{3,2,1,0:T(8,128)} copy(f32[26,4,16,128]{3,2,1,0:T(8,128)} %get-tuple-element.4) | data formatting | bytes 1703936
  42.6 0.0 copy-done
  42.6 0.6 %copy.15 = f32[32,128]{1,0:T(8,128)} copy(f32[32,128]{1,0:T(8,128)S(1)} %copy-done) | data formatting | bytes 32768
Async XLA Ops:
  40.5 2.2 %copy-start = (f32[32,128]{1,0:T(8,128)S(1)}, f32[32,128]{1,0:T(8,128)}, u32[]{:S(2)}) copy-start(f32[32,128]{1,0:T(8,128)} %get-tuple-element.5) | copy-start | bytes 49156
where the time goes:
time: 43.4 us; the launch traced here: 43.2 us
  Pallas kernels  38.5 us (89%)
  local copies, waits for them, and re-layouts  4.09 us (9%)
  between operations  0.65 us (1%)
    pallas_call x1, Pallas kernels, on_device(): pl.pallas_call(functools.partial(body, (nx, ny, height, ex, ey, blocks, c...  38.5 us
    unnamed x5, local copies, waits for them, and re-layouts  4.09 us

commit v1 on v0

--- a/solution.py
+++ b/solution.py
@@ -77,6 +77,16 @@
 def body(
     sizes,
     f_hbm,
+    rho_hbm,
+    speed_hbm,
+    kelvin_hbm,
+    obstacle_hbm,
+    surface_hbm,
+    porosity_hbm,
+    patch_hbm,
+    holder_hbm,
+    out_hbm,
+    tiles_ref,
     rho_ref,
     speed_ref,
     kelvin_ref,
@@ -85,8 +95,6 @@
     porosity_ref,
     patch_ref,
     holder_ref,
-    out_hbm,
-    tiles_ref,
     state,
     const,
     acc,
@@ -119,8 +127,25 @@
     j = lax.axis_index("gy")
     tiles_of = ex // 8
 
-    load = pltpu.make_async_copy(f_hbm, state.at[0, :, :, pl.ds(PAD, ex), :], load_sem)
+    load = pltpu.make_async_copy(f_hbm, state.at[0, :, :, pl.ds(PAD, ex), :], load_sem.at[8])
+    loads = [
+        pltpu.make_async_copy(source, target, load_sem.at[n])
+        for n, (source, target) in enumerate(
+            (
+                (rho_hbm, rho_ref),
+                (speed_hbm, speed_ref),
+                (kelvin_hbm, kelvin_ref),
+                (obstacle_hbm, obstacle_ref),
+                (surface_hbm, surface_ref),
+                (porosity_hbm, porosity_ref),
+                (patch_hbm, patch_ref),
+                (holder_hbm, holder_ref),
+            )
+        )
+    ]
     load.start()
+    for copy in loads:
+        copy.start()
 
     barrier = pltpu.get_barrier_semaphore()
 
@@ -138,13 +163,18 @@
         @pl.when(inside(dx, dy))
         def _():
             pl.semaphore_signal(barrier, inc=1, device_id=(i + dx, j + dy), device_id_type=MESH)
-    for d in range(1, nx):
-        pl.semaphore_signal(barrier, inc=1, device_id=(lax.rem(i + d, nx), j), device_id_type=MESH)
-    for target in mirrors:
-        pl.semaphore_signal(barrier, inc=1, device_id=target, device_id_type=MESH)
+    far = max(nx, ny) - 1 > STEPS + 1
+    if far:
+        for d in range(1, nx):
+            target = (lax.rem(i + d, nx), j)
+            pl.semaphore_signal(barrier, inc=1, device_id=target, device_id_type=MESH)
+        for target in mirrors:
+            pl.semaphore_signal(barrier, inc=1, device_id=target, device_id_type=MESH)
 
     lane = lax.broadcasted_iota(jnp.int32, (8, ey), 1)
 
+    for copy in loads:
+        copy.wait()
     for z in range(height):
         fluid = 1.0 - obstacle_ref[z].astype(jnp.float32)
         for axis in range(3):
@@ -155,7 +185,7 @@
 
     wide = 1 + (i > 0).astype(jnp.int32) + (i < nx - 1).astype(jnp.int32)
     deep = 1 + (j > 0).astype(jnp.int32) + (j < ny - 1).astype(jnp.int32)
-    pl.semaphore_wait(barrier, wide * deep - 1 + nx - 1 + len(mirrors))
+    pl.semaphore_wait(barrier, wide * deep - 1 + (nx - 1 + len(mirrors) if far else 0))
     load.wait()
 
     def rim_copy(par, k):
@@ -176,16 +206,6 @@
         )
 
     def send_rim(par):
-        for side in range(2):
-            row = PAD if side == 0 else PAD + ex - 1
-            for p, pop in enumerate(XPOPS[side]):
-                for z in range(height):
-                    q = p * height + z
-                    xsend[par, side, q : q + 1, :] = state[par, pop, z, row : row + 1, :]
-        for k in range(2):
-            @pl.when(inside(*DIRS[k]))
-            def _():
-                rim_copy(par, k).start()
         for side in range(2):
             for rt in range(tiles_of):
                 packed = jnp.zeros((8, ey), jnp.float32)
@@ -213,6 +233,16 @@
             @pl.when(inside(*DIRS[k]))
             def _():
                 rim_copy(par, k).start()
+        for side in range(2):
+            row = PAD if side == 0 else PAD + ex - 1
+            for p, pop in enumerate(XPOPS[side]):
+                for z in range(height):
+                    q = p * height + z
+                    xsend[par, side, q : q + 1, :] = state[par, pop, z, row : row + 1, :]
+        for k in range(2):
+            @pl.when(inside(*DIRS[k]))
+            def _():
+                rim_copy(par, k).start()
 
     def take_rim(par):
         for k in range(8):
@@ -353,11 +383,17 @@
 
     design = gathered(porosity_ref[...])
 
-    owner = jnp.broadcast_to(holder_ref[...], (blocks, TILE)).astype(jnp.float32)
+    owner_row = jnp.concatenate(
+        [
+            holder_ref[...].astype(jnp.float32),
+            jnp.zeros((1, TILE - blocks), jnp.float32),
+        ],
+        axis=1,
+    )
     rows_of = lax.broadcasted_iota(jnp.int32, (blocks, TILE), 0)
     lanes_of = lax.broadcasted_iota(jnp.int32, (blocks, TILE), 1)
     diagonal = (rows_of == lanes_of).astype(jnp.float32)
-    owner_row = jnp.sum(owner * diagonal, axis=0, keepdims=True)
+    owner = jnp.sum(owner_row * diagonal, axis=1, keepdims=True)
     same = ((owner == owner_row) & (rows_of < lanes_of) & (lanes_of < blocks)).astype(jnp.float32)
     rank_row = jnp.sum(same, axis=0, keepdims=True)
     slot_row = owner_row * float(cap) + rank_row
@@ -487,9 +523,17 @@
             jax.ShapeDtypeStruct(dual_distributions.shape, f32),
             jax.ShapeDtypeStruct((nx * cap, TILE), f32),
         ),
-        in_specs=[hbm] + [vmem] * 8,
+        in_specs=[hbm] * 9,
         out_specs=(hbm, vmem),
         scratch_shapes=[
+            pltpu.VMEM(primal_fluid_rho.shape, f32),
+            pltpu.VMEM(forward_flow_speed.shape, f32),
+            pltpu.VMEM(primal_kelvin_values.shape, f32),
+            pltpu.VMEM(obstacle_mask.shape, jnp.int32),
+            pltpu.VMEM(objective_surface_mask.shape, jnp.int32),
+            pltpu.VMEM(pillar_porosity.shape, f32),
+            pltpu.VMEM(pillar_design_patch.shape, jnp.int32),
+            pltpu.VMEM((1, blocks), jnp.int32),
             pltpu.VMEM((2, pops, height, ex + 2 * PAD, ey), f32),
             pltpu.VMEM((6, height, ex, ey), f32),
             pltpu.VMEM((ex, ey), f32),
@@ -508,7 +552,7 @@
             pltpu.VMEM((3, ex, ey), f32),
             pltpu.VMEM((nx, cap, TILE), f32),
             pltpu.VMEM((nx, cap, TILE), f32),
-            pltpu.SemaphoreType.DMA,
+            pltpu.SemaphoreType.DMA((9,)),
             pltpu.SemaphoreType.DMA,
             pltpu.SemaphoreType.DMA((2, 8)),
             pltpu.SemaphoreType.DMA((2, 8)),
@@ -527,7 +571,7 @@
         objective_surface_mask,
         pillar_porosity,
         pillar_design_patch,
-        patch_holder,
+        patch_holder.T,
     )
 
 

time: 43.4 us -> 40.1 us (0.924)
  Pallas kernels: 38.5 us -> 36.5 us
  local copies, waits for them, and re-layouts: 4.09 us -> 2.76 us
    pallas_call x1, Pallas kernels: 38.5 us -> 36.5 us  [on_device(): pl.pallas_call(functools.partial(body, (nx, ny, height, ex, ey, blocks, c...]
    unnamed x5 -> x4, local copies, waits for them, and re-layouts: 4.09 us -> 2.76 us
where the time goes in v1:
time: 40.1 us; the launch traced here: 39.9 us
  Pallas kernels  36.5 us (91%)
  local copies, waits for them, and re-layouts  2.76 us (7%)
  between operations  0.65 us (2%)
    pallas_call x1, Pallas kernels, on_device(): pl.pallas_call(functools.partial(body, (nx, ny, height, ex, ey, blocks, c...  36.5 us
    unnamed x4, local copies, waits for them, and re-layouts  2.76 us

profile of v1, /device:TPU:0, one launch (start us, length us, event | category | flops | bytes accessed | tf_op | source)
XLA Modules:
  0.0 39.9 jit_solution(10906308801943497405)
XLA Ops:
  0.6 36.5 %shard_map.104 = (f32[26,4,16,128]{3,2,1,0:T(8,128)}, f32[32,128]{1,0:T(8,128)}) custom-call(f32[26,4,16,128]{3,2,1,0:T(8,128)} %f_hbm.1, f32[4,16,128]{2,1,0:T(8,128)} %rho_hbm.1, f32[3,4,16,128]{3,2,1,0:T(8,128)} %speed_hbm.1, f32[4,16,128]{2,1,0:T(8,128)} %kelvin_hbm.1, s32[4,16,128]{2,1,0:T(8,128)} %obstacle_hbm.1, s32[4,16,128]{2,1,0:T(8,128)} %surface_hbm.1, ...), custom_call_target="tpu_custom_call" | custom-call | tf_op jit(solution)/shard_map/pallas_call | solution.py:520
  37.2 0.0 copy-start
  37.2 2.1 %copy.13 = f32[26,4,16,128]{3,2,1,0:T(8,128)} copy(f32[26,4,16,128]{3,2,1,0:T(8,128)} %get-tuple-element.4) | data formatting | bytes 1703936
  39.3 0.0 copy-done
  39.3 0.6 %copy.14 = f32[32,128]{1,0:T(8,128)} copy(f32[32,128]{1,0:T(8,128)S(1)} %copy-done) | data formatting | bytes 32768
Async XLA Ops:
  37.2 2.2 %copy-start = (f32[32,128]{1,0:T(8,128)S(1)}, f32[32,128]{1,0:T(8,128)}, u32[]{:S(2)}) copy-start(f32[32,128]{1,0:T(8,128)} %get-tuple-element.5) | copy-start | bytes 49156

commit v2 on v1

--- a/solution.py
+++ b/solution.py
@@ -85,7 +85,7 @@
     porosity_hbm,
     patch_hbm,
     holder_hbm,
-    out_hbm,
+    out_ref,
     tiles_ref,
     rho_ref,
     speed_ref,
@@ -114,7 +114,6 @@
     outgoing,
     received,
     load_sem,
-    store_sem,
     send_sem,
     recv_sem,
     msend_sem,
@@ -267,7 +266,7 @@
             row = PAD + ex if dx < 0 else PAD - 1
             yhalo[0 if dy < 0 else 1, row : row + 1, :] = crecv[par, k - 4]
 
-    def collide(par, z, rt):
+    def collide(par, z, rt, put, moments_only=False):
         start = PAD + rt * 8
 
         def pull(pop):
@@ -299,15 +298,19 @@
         qx, qy, qz = V1 * (b[1] - b[2]), V1 * (b[3] - b[4]), V1 * (b[5] - b[6])
         qu = qx * ux + qy * uy + qz * uz
         warm = CONDUCT_RATE * (tsum + 4.0 * qu) + source
-        for k in range(7):
-            state[1 - par, FLOW + k, z, start : start + 8, :] = (1.0 - CONDUCT_RATE) * b[k] + warm
-
-        a = [pull(k) for k in range(FLOW)]
+        if not moments_only:
+            for k in range(7):
+                put(FLOW + k, z, rt, (1.0 - CONDUCT_RATE) * b[k] + warm)
+
+        a = [None if moments_only and k == 0 else pull(k) for k in range(FLOW)]
         sm = {k: a[k] + a[k + 1] for k in range(1, FLOW, 2)}
         df = {k: a[k] - a[k + 1] for k in range(1, FLOW, 2)}
         sx = (3.0 * W1) * df[1] + (3.0 * W2) * ((df[7] + df[9]) + (df[11] + df[13]))
         sy = (3.0 * W1) * df[3] + (3.0 * W2) * ((df[7] - df[9]) + (df[15] + df[17]))
         sz = (3.0 * W1) * df[5] + (3.0 * W2) * ((df[11] - df[13]) + (df[15] - df[17]))
+        sens = HEAT_RATE * tsum - rho_ref[z, rows, :] * (ux * sx + uy * sy + uz * sz)
+        if moments_only:
+            return sens
         xy, xz, yz = sm[7] + sm[9], sm[11] + sm[13], sm[15] + sm[17]
         mass = W0 * a[0] + W1 * (sm[1] + sm[3] + sm[5]) + W2 * (xy + xz + yz)
         quad = (
@@ -340,14 +343,11 @@
         }
         keep = 1.0 - OMEGA_FLOW
 
-        def put(pop, value):
-            state[1 - par, pop, z, start : start + 8, :] = value
-
-        put(0, jnp.where(fluid, keep * a[0] + base, a[0]))
+        put(0, z, rt, jnp.where(fluid, keep * a[0] + base, a[0]))
         for k in range(1, FLOW, 2):
-            put(k, jnp.where(fluid, keep * a[k] + (base + along[k]), a[k + 1]))
-            put(k + 1, jnp.where(fluid, keep * a[k + 1] + (base - along[k]), a[k]))
-        return HEAT_RATE * tsum - rho_ref[z, rows, :] * (ux * sx + uy * sy + uz * sz)
+            put(k, z, rt, jnp.where(fluid, keep * a[k] + (base + along[k]), a[k + 1]))
+            put(k + 1, z, rt, jnp.where(fluid, keep * a[k + 1] + (base - along[k]), a[k]))
+        return sens
 
     send_rim(0)
 
@@ -405,26 +405,33 @@
 
     def step(s, carry):
         par = lax.rem(s, 2)
+
+        def put(pop, z, rt, value):
+            start = PAD + rt * 8
+            state[1 - par, pop, z, start : start + 8, :] = value
+
         take_rim(par)
         for rt in range(tiles_of):
-            sens = collide(par, 0, rt)
+            sens = collide(par, 0, rt, put)
             for z in range(1, height):
-                sens = sens + collide(par, z, rt)
+                sens = sens + collide(par, z, rt, put)
             acc[rt * 8 : rt * 8 + 8, :] += sens
-
-        @pl.when(s < STEPS - 1)
-        def _():
-            send_rim(1 - par)
-
+        send_rim(1 - par)
         return carry
 
-    lax.fori_loop(0, STEPS, step, 0)
-
-    last = STEPS % 2
-    store = pltpu.make_async_copy(state.at[last, :, :, pl.ds(PAD, ex), :], out_hbm, store_sem)
-    store.start()
-
-    column[...] = acc[...]
+    lax.fori_loop(0, STEPS - 1, step, 0)
+
+    last = (STEPS - 1) % 2
+
+    def put_out(pop, z, rt, value):
+        out_ref[pop, z, rt * 8 : rt * 8 + 8, :] = value
+
+    take_rim(last)
+    for rt in range(tiles_of):
+        sens = collide(last, 0, rt, None, True)
+        for z in range(1, height):
+            sens = sens + collide(last, z, rt, None, True)
+        column[rt * 8 : rt * 8 + 8, :] = acc[rt * 8 : rt * 8 + 8, :] + sens
 
     def mirror_copy(m):
         return pltpu.make_async_remote_copy(
@@ -438,6 +445,9 @@
 
     for m in (2, 1, 0):
         mirror_copy(m).start()
+    for rt in range(tiles_of):
+        for z in range(height):
+            collide(last, z, rt, put_out)
     for m in range(3):
         mirror_copy(m).wait()
     for x in range(ex):
@@ -495,7 +505,6 @@
         arriving(d).wait_recv()
     for o in range(nx):
         tiles_ref[o * cap : (o + 1) * cap, :] = received[o]
-    store.wait()
 
 
 def on_device(
@@ -520,11 +529,11 @@
     return pl.pallas_call(
         functools.partial(body, (nx, ny, height, ex, ey, blocks, cap)),
         out_shape=(
-            jax.ShapeDtypeStruct(dual_distributions.shape, f32),
-            jax.ShapeDtypeStruct((nx * cap, TILE), f32),
+            pltpu.VMEM(dual_distributions.shape, f32),
+            pltpu.VMEM((nx * cap, TILE), f32),
         ),
         in_specs=[hbm] * 9,
-        out_specs=(hbm, vmem),
+        out_specs=(vmem, vmem),
         scratch_shapes=[
             pltpu.VMEM(primal_fluid_rho.shape, f32),
             pltpu.VMEM(forward_flow_speed.shape, f32),
@@ -553,7 +562,6 @@
             pltpu.VMEM((nx, cap, TILE), f32),
             pltpu.VMEM((nx, cap, TILE), f32),
             pltpu.SemaphoreType.DMA((9,)),
-            pltpu.SemaphoreType.DMA,
             pltpu.SemaphoreType.DMA((2, 8)),
             pltpu.SemaphoreType.DMA((2, 8)),
             pltpu.SemaphoreType.DMA((3,)),

time: 40.1 us -> 37.5 us (0.935)
  Pallas kernels: 36.5 us -> 35.2 us
  local copies, waits for them, and re-layouts: 2.76 us -> 1.51 us
    pallas_call x1, Pallas kernels: 36.5 us -> 35.2 us  [on_device(): pl.pallas_call(functools.partial(body, (nx, ny, height, ex, ey, blocks, c...]
    unnamed x4 -> x2, local copies, waits for them, and re-layouts: 2.76 us -> 1.51 us
where the time goes in v2:
time: 37.5 us; the launch traced here: 37.4 us
  Pallas kernels  35.2 us (94%)
  local copies, waits for them, and re-layouts  1.51 us (4%)
  between operations  0.64 us (2%)
    pallas_call x1, Pallas kernels, on_device(): pl.pallas_call(functools.partial(body, (nx, ny, height, ex, ey, blocks, c...  35.2 us
    unnamed x2, local copies, waits for them, and re-layouts  1.51 us

profile of v2, /device:TPU:0, one launch (start us, length us, event | category | flops | bytes accessed | tf_op | source)
XLA Modules:
  0.0 37.4 jit_solution(17584052339743836411)
XLA Ops:
  0.6 35.2 %shard_map.104 = (f32[26,4,16,128]{3,2,1,0:T(8,128)S(1)}, f32[32,128]{1,0:T(8,128)S(1)}) custom-call(f32[26,4,16,128]{3,2,1,0:T(8,128)} %f_hbm.1, f32[4,16,128]{2,1,0:T(8,128)} %rho_hbm.1, f32[3,4,16,128]{3,2,1,0:T(8,128)} %speed_hbm.1, f32[4,16,128]{2,1,0:T(8,128)} %kelvin_hbm.1, s32[4,16,128]{2,1,0:T(8,128)} %obstacle_hbm.1, s32[4,16,128]{2,1,0:T(8,128)} %surface_hbm.1, ...), custom_call_target="tpu_custom_call" | custom-call | tf_op jit(solution)/shard_map/pallas_call | solution.py:529
  35.9 0.9 %copy.13 = f32[26,4,16,128]{3,2,1,0:T(8,128)} copy(f32[26,4,16,128]{3,2,1,0:T(8,128)S(1)} %get-tuple-element.2) | data formatting | bytes 1703936
  36.8 0.6 %copy.14 = f32[32,128]{1,0:T(8,128)} copy(f32[32,128]{1,0:T(8,128)S(1)} %get-tuple-element.3) | data formatting | bytes 32768

commit v3 on v2

--- a/solution.py
+++ b/solution.py
@@ -244,27 +244,32 @@
                 rim_copy(par, k).start()
 
     def take_rim(par):
-        for k in range(8):
+        def arrived(k):
             dx, dy = DIRS[k]
-
-            @pl.when(inside(dx, dy))
-            def _():
-                rim_copy(par, k).wait_send()
 
             @pl.when(inside(-dx, -dy))
             def _():
                 rim_copy(par, k).wait_recv()
+
         for side in range(2):
+            arrived(side)
             row = PAD + ex if side == 0 else PAD - 1
             for p, pop in enumerate(XPOPS[side]):
                 for z in range(height):
                     q = p * height + z
                     state[par, pop, z, row : row + 1, :] = xrecv[par, side, q : q + 1, :]
+        for side in range(2):
+            arrived(2 + side)
             yhalo[side, PAD : PAD + ex, :] = yrecv[par, side]
         for k in range(4, 8):
+            arrived(k)
             dx, dy = DIRS[k]
             row = PAD + ex if dx < 0 else PAD - 1
             yhalo[0 if dy < 0 else 1, row : row + 1, :] = crecv[par, k - 4]
+        for k in range(8):
+            @pl.when(inside(*DIRS[k]))
+            def _():
+                rim_copy(par, k).wait_send()
 
     def collide(par, z, rt, put, moments_only=False):
         start = PAD + rt * 8

time: 37.5 us -> 37.6 us (level)
  no operation moved by 1% of the time
where the time goes in v3:
time: 37.6 us; the launch traced here: 37.4 us
  Pallas kernels  35.3 us (94%)
  local copies, waits for them, and re-layouts  1.51 us (4%)
  between operations  0.64 us (2%)
    pallas_call x1, Pallas kernels, on_device(): pl.pallas_call(functools.partial(body, (nx, ny, height, ex, ey, blocks, c...  35.3 us
    unnamed x2, local copies, waits for them, and re-layouts  1.51 us

profile of v3, /device:TPU:0, one launch (start us, length us, event | category | flops | bytes accessed | tf_op | source)
XLA Modules:
  0.0 37.4 jit_solution(16448501918362780975)
XLA Ops:
  0.6 35.3 %shard_map.104 = (f32[26,4,16,128]{3,2,1,0:T(8,128)S(1)}, f32[32,128]{1,0:T(8,128)S(1)}) custom-call(f32[26,4,16,128]{3,2,1,0:T(8,128)} %f_hbm.1, f32[4,16,128]{2,1,0:T(8,128)} %rho_hbm.1, f32[3,4,16,128]{3,2,1,0:T(8,128)} %speed_hbm.1, f32[4,16,128]{2,1,0:T(8,128)} %kelvin_hbm.1, s32[4,16,128]{2,1,0:T(8,128)} %obstacle_hbm.1, s32[4,16,128]{2,1,0:T(8,128)} %surface_hbm.1, ...), custom_call_target="tpu_custom_call" | custom-call | tf_op jit(solution)/shard_map/pallas_call | solution.py:534
  35.9 0.9 %copy.13 = f32[26,4,16,128]{3,2,1,0:T(8,128)} copy(f32[26,4,16,128]{3,2,1,0:T(8,128)S(1)} %get-tuple-element.2) | data formatting | bytes 1703936
  36.8 0.6 %copy.14 = f32[32,128]{1,0:T(8,128)} copy(f32[32,128]{1,0:T(8,128)S(1)} %get-tuple-element.3) | data formatting | bytes 32768
